TPU v7x, 32 devices: a whole 2x2x4 slice. The times are simulated.
32 devices in a mesh: shard: 8 (over z, x), tensor: 4 (over y, core).
Axes of the slice: x: 2, y: 2, z: 4, core: 2. Of those that a mesh axis runs over, the one named last changes fastest.
Arguments:
- matrix_grads: bfloat16 [56, 512, 2560], P(None, 'shard', 'tensor'), may hold values from -64 to 64
- matrix_momentum: float32 [56, 512, 2560], P(None, 'shard', 'tensor'), may hold values from -64 to 64
- matrix_weights: float32 [56, 512, 2560], P(None, 'shard', 'tensor'), may hold values from -6 to 6
- table_grads: bfloat16 [2048, 2560], P('shard', 'tensor'), may hold values from -6 to 6
- table_state: float32 [3, 2048, 2560], P(None, 'shard', 'tensor'), may hold values from -4 to 4, as said below
- small_grads: bfloat16 [120, 2560], P(None, 'tensor'), may hold values from -6 to 6
- small_state: float32 [3, 120, 2560], P(None, None, 'tensor'), may hold values from -4 to 4, as said below
Outputs:
- matrix_update: float32 [56, 512, 2560], P(None, 'shard', 'tensor')
- momentum_next: float32 [56, 512, 2560], P(None, 'shard', 'tensor')
- table_out: float32 [2, 2048, 2560], P(None, 'shard', 'tensor')
- small_out: float32 [2, 120, 2560], P(None, None, 'tensor')
Inputs may be any that keep to these rules, and one draw needn't show every extreme that they name: `table_state`: index 0 holds weights, index 1 first moments, index 2 second moments, which lie between 0.0002 and 0.004. `small_state`: index 0 holds weights, index 1 first moments, index 2 second moments, which lie between 0.0002 and 0.004.
All inputs are finite; a program needn't handle non-finite values.
Results may differ from a plain program's by a relative error of at most 0.014.
The roundings to bfloat16 on the way count: a program that leaves them out, or rounds other values in their place, can miss the bound.
Values may be sent and summed in bfloat16 or wider, within the bound.
A program may use at most 192 MiB of HBM per device.

v0:
```python
import math
import jax
import jax.numpy as jnp
from jax import lax
from jax.sharding import PartitionSpec as P

D = 2560
KV = 512
EXPERTS = 64
ITERS = 5
COEF_A = 3.4445
COEF_B = -4.775
COEF_C = 2.0315
BIAS_ONE = 1.0 - 0.9**10
BIAS_TWO = 1.0 - 0.999**10


def unchanged(values):
    return values


def newton_schulz(blended, square_total, gram_total):
    squares = square_total(jnp.sum(jnp.square(blended.astype(jnp.float32)), axis=(1, 2)))
    iterate = (blended.astype(jnp.float32) / (jnp.sqrt(squares) + 1e-07)[:, None, None]).astype(
        jnp.bfloat16
    )
    iterate = lax.optimization_barrier(iterate)
    for turn in range(ITERS):
        gram_term = jnp.einsum("krc,ksc->krs", iterate, iterate, preferred_element_type=jnp.float32)
        gram_matrix = gram_total(gram_term).astype(jnp.bfloat16)
        gram_matrix = lax.optimization_barrier(gram_matrix)
        gram_square = jnp.einsum(
            "krs,kst->krt", gram_matrix, gram_matrix, preferred_element_type=jnp.float32
        )
        polynomial = (COEF_B * gram_matrix.astype(jnp.float32) + COEF_C * gram_square).astype(
            jnp.bfloat16
        )
        product = jnp.einsum(
            "krs,ksc->krc", polynomial, iterate, preferred_element_type=jnp.float32
        )
        iterate = (COEF_A * iterate.astype(jnp.float32) + product).astype(jnp.bfloat16)
        iterate = lax.optimization_barrier(iterate)
    return iterate


def pad_matrices(blended, total):
    extra = total - blended.shape[0]
    filler = jnp.zeros((extra,) + blended.shape[1:], blended.dtype)
    return jnp.concatenate([blended, filler], axis=0)


def adamw(gradient, states, decay_rate):
    grad_value = gradient.astype(jnp.float32)
    moment_one = 0.9 * states[1] + 0.1 * grad_value
    moment_two = 0.999 * states[2] + 0.001 * grad_value * grad_value
    direction = (
        moment_one / BIAS_ONE / (jnp.sqrt(moment_two / BIAS_TWO) + 1e-08) + decay_rate * states[0]
    )
    return jnp.stack([direction, moment_one])


def local(
    matrix_grads,
    matrix_momentum,
    matrix_weights,
    table_grads,
    table_state,
    small_grads,
    small_state,
):
    momentum_next = 0.95 * matrix_momentum + matrix_grads.astype(jnp.float32)
    blended = (matrix_grads.astype(jnp.float32) + 0.95 * momentum_next).astype(jnp.bfloat16)
    matrix_count, rows_local, cols_local = blended.shape
    shards = lax.axis_size("shard")
    tensor_size = lax.axis_size("tensor")
    devices = shards * tensor_size
    per_device = -(-matrix_count // devices)
    padded = pad_matrices(blended, per_device * devices)
    source = padded.reshape(shards, tensor_size, per_device, rows_local, cols_local)
    arrived = lax.all_to_all(
        lax.all_to_all(source, "shard", split_axis=0, concat_axis=3, tiled=True),
        "tensor",
        split_axis=1,
        concat_axis=4,
        tiled=True,
    )
    whole_result = newton_schulz(arrived[0, 0], unchanged, unchanged)
    returned = lax.all_to_all(
        lax.all_to_all(whole_result[None, None], "shard", split_axis=3, concat_axis=0, tiled=True),
        "tensor",
        split_axis=4,
        concat_axis=1,
        tiled=True,
    )
    orthogonal = returned.reshape(devices * per_device, rows_local, cols_local)[:matrix_count]
    muon_scale = 0.2 * math.sqrt(max(KV, D))
    matrix_update = muon_scale * orthogonal.astype(jnp.float32) + 0.1 * matrix_weights
    table_out = adamw(table_grads, table_state, 0.1)
    row_index = jnp.arange(small_grads.shape[0], dtype=jnp.int32)
    small_decay = jnp.where(row_index < EXPERTS, 0.1, 0.0).astype(jnp.float32)[:, None]
    small_out = adamw(small_grads, small_state, small_decay)
    return (matrix_update, momentum_next, table_out, small_out)


def solution(mesh):
    placed = (
        P(None, "shard", "tensor"),
        P(None, "shard", "tensor"),
        P(None, "shard", "tensor"),
        P("shard", "tensor"),
        P(None, "shard", "tensor"),
        P(None, "tensor"),
        P(None, None, "tensor"),
    )
    return jax.shard_map(
        local,
        mesh=mesh,
        in_specs=placed,
        out_specs=(
            P(None, "shard", "tensor"),
            P(None, "shard", "tensor"),
            P(None, "shard", "tensor"),
            P(None, None, "tensor"),
        ),
        check_vma=False,
    )
```

profile of v0, /device:TPU:0, one launch (start us, length us, event | category | flops | bytes accessed | tf_op | source)
XLA Modules:
  0.0 594.8 jit_solution(7325919482131494463)
XLA Ops:
  0.6 12.7 %fusion.1 = (bf16[56,64,640]{2,1,0:T(8,128)(2,1)}, f32[56,64,640]{2,1,0:T(8,128)}) fusion(bf16[56,64,640]{2,1,0:T(8,128)(2,1)} %param.7, f32[56,64,640]{2,1,0:T(8,128)} %param.8), kind=kLoop, calls=%fused_computation.11 | loop fusion | flops 13762560 | bytes 27525120 | tf_op jit(solution)/shard_map/convert_element_type | solution.py:72
  13.3 3.0 concatenate.3
  16.3 122.7 %all_to_all.60 = bf16[8,4,2,64,640]{4,3,2,1,0:T(8,128)(2,1)S(1)} all-to-all(bf16[8,4,2,64,640]{4,3,2,1,0:T(8,128)(2,1)S(1)} %bitcast.89), channel_id=1, replica_groups=mesh['shard'=8,'tensor'=4] {'shard'}, dimensions={0} | all-to-all | bytes 10485760 | tf_op jit(solution)/shard_map/all_to_all | solution.py:81
  139.0 0.6 copy.33
  139.6 62.5 %all_to_all.61 = bf16[1,4,2,512,640]{4,3,2,0,1:T(8,128)(2,1)S(1)} all-to-all(bf16[1,4,2,512,640]{4,3,2,0,1:T(8,128)(2,1)S(1)} %bitcast.90), channel_id=1, replica_groups=mesh['shard'=8,'tensor'=4] {'tensor'}, dimensions={1} | all-to-all | bytes 10485760 | tf_op jit(solution)/shard_map/all_to_all | solution.py:80
  202.1 1.5 fusion
  203.6 4.5 convert_bitcast_fusion
  208.2 14.7 %copy.35 = f32[1,1,2,512,4,640]{5,4,3,2,1,0:T(4,128)} copy(f32[1,1,2,512,4,640]{5,3,2,4,1,0:T(8,128)} %convert_bitcast_fusion) | data formatting | bytes 20971520 | tf_op jit(solution)/shard_map/convert_element_type | solution.py:24
  222.8 13.0 %reshape.44 = f32[2,512,2560]{2,1,0:T(8,128)} reshape(f32[1,1,2,512,4,640]{5,4,3,2,1,0:T(4,128)} %copy.35) | data formatting | bytes 20971520 | tf_op jit(solution)/shard_map/convert_element_type | solution.py:24
  235.8 5.3 divide_convert_fusion
  241.1 0.0 copy-start
  241.1 2.3 copy-done
  243.5 2.9 convolution_convert_fusion.4
  246.4 8.5 %add_convert_fusion.4 = bf16[2,512,2560]{2,1,0:T(8,128)(2,1)} fusion(bf16[2,512,2560]{2,1,0:T(8,128)(2,1)} %copy-done, bf16[2,512,512]{2,1,0:T(8,128)(2,1)S(1)} %convolution_convert_fusion.4), kind=kOutput, calls=%fused_computation.9 | convolution fusion | flops 3234332672 | bytes 11534336 | tf_op jit(solution)/shard_map/krs,ksc->krc/dot_general | solution.py:38
  254.9 6.9 %convolution_convert_fusion.3 = bf16[2,512,512]{2,1,0:T(8,128)(2,1)S(1)} fusion(bf16[2,512,2560]{2,1,0:T(8,128)(2,1)} %add_convert_fusion.4), kind=kOutput, calls=%fused_computation.22 | convolution fusion | flops 2684878848 | bytes 6291456 | tf_op jit(solution)/shard_map/krc,ksc->krs/dot_general | solution.py:29
  261.8 8.4 %add_convert_fusion.3 = bf16[2,512,2560]{2,1,0:T(8,128)(2,1)} fusion(bf16[2,512,2560]{2,1,0:T(8,128)(2,1)} %add_convert_fusion.4, bf16[2,512,512]{2,1,0:T(8,128)(2,1)S(1)} %convolution_convert_fusion.3), kind=kOutput, calls=%fused_computation.8 | convolution fusion | flops 3234332672 | bytes 11534336 | tf_op jit(solution)/shard_map/krs,ksc->krc/dot_general | solution.py:38
  270.2 6.9 %convolution_convert_fusion.2 = bf16[2,512,512]{2,1,0:T(8,128)(2,1)S(1)} fusion(bf16[2,512,2560]{2,1,0:T(8,128)(2,1)} %add_convert_fusion.3), kind=kOutput, calls=%fused_computation.21 | convolution fusion | flops 2684878848 | bytes 6291456 | tf_op jit(solution)/shard_map/krc,ksc->krs/dot_general | solution.py:29
  277.2 8.7 %add_convert_fusion.2 = bf16[2,512,2560]{2,1,0:T(8,128)(2,1)} fusion(bf16[2,512,2560]{2,1,0:T(8,128)(2,1)} %add_convert_fusion.3, bf16[2,512,512]{2,1,0:T(8,128)(2,1)S(1)} %convolution_convert_fusion.2), kind=kOutput, calls=%fused_computation.7 | convolution fusion | flops 3234332672 | bytes 11534336 | tf_op jit(solution)/shard_map/krs,ksc->krc/dot_general | solution.py:38
  285.9 6.9 %convolution_convert_fusion.1 = bf16[2,512,512]{2,1,0:T(8,128)(2,1)S(1)} fusion(bf16[2,512,2560]{2,1,0:T(8,128)(2,1)} %add_convert_fusion.2), kind=kOutput, calls=%fused_computation.20 | convolution fusion | flops 2684878848 | bytes 6291456 | tf_op jit(solution)/shard_map/krc,ksc->krs/dot_general | solution.py:29
  292.8 8.4 %add_convert_fusion.1 = bf16[2,512,2560]{2,1,0:T(8,128)(2,1)} fusion(bf16[2,512,2560]{2,1,0:T(8,128)(2,1)} %add_convert_fusion.2, bf16[2,512,512]{2,1,0:T(8,128)(2,1)S(1)} %convolution_convert_fusion.1), kind=kOutput, calls=%fused_computation.6 | convolution fusion | flops 3234332672 | bytes 11534336 | tf_op jit(solution)/shard_map/krs,ksc->krc/dot_general | solution.py:38
  301.3 6.9 %convolution_convert_fusion = bf16[2,512,512]{2,1,0:T(8,128)(2,1)S(1)} fusion(bf16[2,512,2560]{2,1,0:T(8,128)(2,1)} %add_convert_fusion.1), kind=kOutput, calls=%fused_computation.19 | convolution fusion | flops 2684878848 | bytes 6291456 | tf_op jit(solution)/shard_map/krc,ksc->krs/dot_general | solution.py:29
  308.2 8.7 %add_convert_fusion = bf16[2,512,2560]{2,1,0:T(8,128)(2,1)} fusion(bf16[2,512,2560]{2,1,0:T(8,128)(2,1)} %add_convert_fusion.1, bf16[2,512,512]{2,1,0:T(8,128)(2,1)S(1)} %convolution_convert_fusion), kind=kOutput, calls=%fused_computation.5 | convolution fusion | flops 3234332672 | bytes 11534336 | tf_op jit(solution)/shard_map/krs,ksc->krc/dot_general | solution.py:38
  316.9 10.2 %copy.36 = bf16[1,1,2,512,2560]{4,2,1,0,3:T(2,128)(2,1)} copy(bf16[1,1,2,512,2560]{4,3,2,1,0:T(8,128)(2,1)} %bitcast.93) | data formatting | bytes 10485760 | tf_op jit(solution)/shard_map/broadcast_in_dim | solution.py:89
  327.2 120.1 %all_to_all.62 = bf16[1,1,2,512,2560]{4,2,1,0,3:T(2,128)(2,1)} all-to-all(bf16[1,1,2,512,2560]{4,2,1,0,3:T(2,128)(2,1)} %copy.36), channel_id=1, replica_groups=mesh['shard'=8,'tensor'=4] {'shard'}, dimensions={3} | all-to-all | bytes 10485760 | tf_op jit(solution)/shard_map/all_to_all | solution.py:89
  447.3 17.4 %copy.37 = bf16[1,1,2,8,64,2560]{4,3,2,5,1,0:T(8,128)(2,1)} copy(bf16[1,1,2,8,64,2560]{5,2,4,3,1,0:T(2,128)(2,1)} %bitcast.91) | data formatting | bytes 10485760 | tf_op jit(solution)/shard_map/all_to_all | solution.py:89
  464.7 10.4 %bitcast_bitcast_fusion = bf16[2560,1,2,8,64]{4,3,2,1,0:T(8,128)(2,1)} fusion(bf16[1,1,2,8,64,2560]{4,3,2,5,1,0:T(8,128)(2,1)} %copy.37), kind=kLoop, calls=%fused_computation.61 | loop fusion | bytes 10485760
  475.0 11.2 %reshape.46 = bf16[4,2,327680]{2,1,0:T(2,128)(2,1)} reshape(bf16[2560,1,2,8,64]{4,3,2,1,0:T(8,128)(2,1)} %bitcast_bitcast_fusion) | data formatting | bytes 10485760
  486.2 0.0 copy-start.2
  486.2 0.0 copy-start.4
  486.2 0.0 copy-start.1
  486.2 0.0 copy-start.3
  486.2 5.6 all-to-all-start.3
  491.9 0.0 copy-done.2
  491.9 0.0 copy-done.4
  491.9 0.2 fusion.18
  492.1 0.9 pad_maximum_fusion.1
  493.0 0.0 copy-done.1
  493.0 0.0 copy-done.3
  493.0 0.5 fusion.9
  493.5 1.1 pad_maximum_fusion
  494.6 56.7 %all-to-all-done.3 = bf16[4,2,327680]{2,1,0:T(2,128)(2,1)} async-done(((bf16[4,2,327680]{2,1,0:T(2,128)(2,1)}), bf16[4,2,327680]{2,1,0:T(2,128)(2,1)}, u32[]{:S(2)}, u32[]{:S(2)}) %all-to-all-start.3) | async-done | bytes 5242912 | tf_op jit(solution)/shard_map/all_to_all | solution.py:88
  551.3 11.0 %reshape.47 = bf16[2560,1,2,8,64]{4,3,2,1,0:T(8,128)(2,1)} reshape(bf16[4,2,327680]{2,1,0:T(2,128)(2,1)} %all-to-all-done.3) | data formatting | bytes 10485760
  562.3 12.7 %copy.39 = bf16[8,1,2,64,4,640]{5,3,2,1,4,0:T(8,128)(2,1)} copy(bf16[8,1,2,64,4,640]{3,0,2,5,4,1:T(8,128)(2,1)} %bitcast.88) | data formatting | bytes 10485760 | tf_op jit(solution)/shard_map/all_to_all | solution.py:88
  575.0 7.1 %convert_multiply_fusion.1 = f32[7,4,1,2,64,640]{5,4,3,2,1,0:T(8,128)} fusion(bf16[8,4,1,2,64,640]{5,4,3,2,1,0:T(8,128)(2,1)} %bitcast.92), kind=kLoop, calls=%fused_computation.13 | loop fusion | flops 4587520 | bytes 13762560 | tf_op jit(solution)/shard_map/mul | solution.py:97
  582.1 12.4 %bitcast_add_fusion = f32[56,64,640]{2,1,0:T(8,128)} fusion(f32[7,4,1,2,64,640]{5,4,3,2,1,0:T(8,128)} %convert_multiply_fusion.1, f32[56,64,640]{2,1,0:T(8,128)} %param.9), kind=kLoop, calls=%fused_computation.12 | loop fusion | flops 4587520 | bytes 27525120 | tf_op jit(solution)/shard_map/add | solution.py:97
  (2 shorter events, 0.0 us)
Async XLA Ops:
  241.1 2.4 copy-start
  486.2 5.7 copy-start.2
  486.2 5.7 copy-start.4
  486.2 6.8 %copy-start.1 = (f32[3,256,640]{2,1,0:T(8,128)S(1)}, f32[3,256,640]{2,1,0:T(8,128)}, u32[]{:S(2)}) copy-start(f32[3,256,640]{2,1,0:T(8,128)} %param.11) | copy-start | bytes 5898244
  486.2 6.8 %copy-start.3 = (bf16[256,640]{1,0:T(8,128)(2,1)S(1)}, bf16[256,640]{1,0:T(8,128)(2,1)}, u32[]{:S(2)}) copy-start(bf16[256,640]{1,0:T(8,128)(2,1)} %param.10) | copy-start | bytes 983044
  486.2 65.1 %all-to-all-start.3 = ((bf16[4,2,327680]{2,1,0:T(2,128)(2,1)}), bf16[4,2,327680]{2,1,0:T(2,128)(2,1)}, u32[]{:S(2)}, u32[]{:S(2)}) async-start(bf16[4,2,327680]{2,1,0:T(2,128)(2,1)} %reshape.46), calls=%async_computation.3 | async-start | bytes 10485760 | tf_op jit(solution)/shard_map/all_to_all | solution.py:88
where the time goes:
time: 599 us; the launch traced here: 595 us
  blocking collectives  305 us (51%)
  local copies, waits for them, and re-layouts  106 us (18%)
  matrix products  73.4 us (12%)
  waiting for transfers between devices  56.7 us (9%)
  other arithmetic  46.2 us (8%)
    all_to_all x1, blocking collectives, local(): lax.all_to_all(source, 'shard', split_axis=0, concat_axis=3, tiled=True)  123 us
    all_to_all x1, blocking collectives, local(): lax.all_to_all(whole_result[None, None], 'shard', split_axis=3, concat_ax...  120 us
    all_to_all x1, blocking collectives, local(): lax.all_to_all(lax.all_to_all(source, 'shard', split_axis=0, concat_axis=...  62.5 us
    all_to_all x1, waiting for transfers between devices, local(): lax.all_to_all(lax.all_to_all(whole_result[None, None], 'shard', split_ax...  56.7 us
    dot_general x5, matrix products, newton_schulz(): jnp.einsum('krs,ksc->krc', polynomial, iterate, preferred_element_type=jn...  42.7 us
    unnamed x13, local copies, waits for them, and re-layouts  34.9 us
    dot_general x5, matrix products, newton_schulz(): jnp.einsum('krc,ksc->krs', iterate, iterate, preferred_element_type=jnp.f...  30.7 us
    convert_element_type x2, local copies, waits for them, and re-layouts, newton_schulz(): blended.astype(jnp.float32) / (jnp.sqrt(squares) + 1e-07)[:, None, None]  27.6 us
  transfers between devices with their start and end apart: 1, of which 1 were waited for; matrix products, arithmetic and copies ran while one was open for 0% of the time, Pallas kernels for 0%

commit v1 on v0

--- a/solution.py
+++ b/solution.py
@@ -13,6 +13,22 @@
 COEF_C = 2.0315
 BIAS_ONE = 1.0 - 0.9**10
 BIAS_TWO = 1.0 - 0.999**10
+
+
+def pairwise_exchange(x, axis, split, join):
+    ways, here = (lax.axis_size(axis), lax.axis_index(axis))
+    width = x.shape[split] // ways
+    dims = list(x.shape)
+    dims[split] = width
+    height = dims[join]
+    dims[join] = height * ways
+    full = jnp.zeros(dims, x.dtype)
+    for mask in range(ways):
+        part = lax.dynamic_slice_in_dim(x, (here ^ mask) * width, width, axis=split)
+        if mask:
+            part = lax.ppermute(part, axis, [(d, d ^ mask) for d in range(ways)])
+        full = lax.dynamic_update_slice_in_dim(full, part, (here ^ mask) * height, axis=join)
+    return full
 
 
 def unchanged(values):
@@ -77,12 +93,8 @@
     per_device = -(-matrix_count // devices)
     padded = pad_matrices(blended, per_device * devices)
     source = padded.reshape(shards, tensor_size, per_device, rows_local, cols_local)
-    arrived = lax.all_to_all(
-        lax.all_to_all(source, "shard", split_axis=0, concat_axis=3, tiled=True),
-        "tensor",
-        split_axis=1,
-        concat_axis=4,
-        tiled=True,
+    arrived = pairwise_exchange(
+        lax.all_to_all(source, "shard", split_axis=0, concat_axis=3, tiled=True), "tensor", 1, 4
     )
     whole_result = newton_schulz(arrived[0, 0], unchanged, unchanged)
     returned = lax.all_to_all(

time: 599 us -> 570 us (0.952)
  blocking collectives: 305 us -> 121 us
  waiting for transfers between devices: 56.7 us -> 226 us
  local copies, waits for them, and re-layouts: 106 us -> 92 us
  starting transfers between devices: 5.62 us -> 15 us
  other arithmetic: 46.2 us -> 37.5 us
    all_to_all x2 -> x0, blocking collectives: 185 us -> none  [the longest x1 123 us: local(): lax.all_to_all(source, 'shard', split_axis=0, concat_axis=3, tiled=True)]
    all_to_all x0 -> x1, waiting for transfers between devices: none -> 116 us  [local(): lax.all_to_all(source, 'shard', split_axis=0, concat_axis=3, tiled=True)]
    ppermute x0 -> x3, waiting for transfers between devices: none -> 53.6 us  [pairwise_exchange(): part = lax.ppermute(part, axis, [(d, d ^ mask) for d in range(ways)])]
    convert_element_type x2 -> x0, local copies, waits for them, and re-layouts: 27.6 us -> none  [newton_schulz(): blended.astype(jnp.float32) / (jnp.sqrt(squares) + 1e-07)[:, None, None]]
    all_to_all x0 -> x1, starting transfers between devices: none -> 7.6 us  [local(): lax.all_to_all(source, 'shard', split_axis=0, concat_axis=3, tiled=True)]
    unnamed x13 -> x15, local copies, waits for them, and re-layouts: 34.9 us -> 37.3 us
  transfers between devices with their start and end apart: 1 -> 5, of which waited for: 1 -> 4; matrix products, arithmetic and copies ran while one was open for 0% -> 1% of each run, Pallas kernels for 0% -> 0%
where the time goes in v1:
time: 570 us; the launch traced here: 566 us
  waiting for transfers between devices  226 us (40%)
  blocking collectives  121 us (21%)
  local copies, waits for them, and re-layouts  92 us (16%)
  matrix products  73.5 us (13%)
  other arithmetic  37.5 us (7%)
  starting transfers between devices  15 us (3%)
    all_to_all x1, blocking collectives, local(): lax.all_to_all(whole_result[None, None], 'shard', split_axis=3, concat_ax...  121 us
    all_to_all x1, waiting for transfers between devices, local(): lax.all_to_all(source, 'shard', split_axis=0, concat_axis=3, tiled=True)  116 us
    all_to_all x1, waiting for transfers between devices, local(): lax.all_to_all(lax.all_to_all(whole_result[None, None], 'shard', split_ax...  56.7 us
    ppermute x3, waiting for transfers between devices, pairwise_exchange(): part = lax.ppermute(part, axis, [(d, d ^ mask) for d in range(ways)])  53.6 us
    dot_general x5, matrix products, newton_schulz(): jnp.einsum('krs,ksc->krc', polynomial, iterate, preferred_element_type=jn...  42.8 us
    unnamed x15, local copies, waits for them, and re-layouts  37.3 us
    dot_general x5, matrix products, newton_schulz(): jnp.einsum('krc,ksc->krs', iterate, iterate, preferred_element_type=jnp.f...  30.7 us
    all_to_all x1, local copies, waits for them, and re-layouts, local(): lax.all_to_all(whole_result[None, None], 'shard', split_axis=3, concat_ax...  17.4 us
  transfers between devices with their start and end apart: 5, of which 4 were waited for; matrix products, arithmetic and copies ran while one was open for 1% of the time, Pallas kernels for 0%

profile of v1, /device:TPU:0, one launch (start us, length us, event | category | flops | bytes accessed | tf_op | source)
XLA Modules:
  0.0 565.7 jit_solution(7635064692515404357)
XLA Ops:
  0.6 12.7 %fusion.2 = (bf16[56,64,640]{2,1,0:T(8,128)(2,1)}, f32[56,64,640]{2,1,0:T(8,128)}) fusion(bf16[56,64,640]{2,1,0:T(8,128)(2,1)} %param.7, f32[56,64,640]{2,1,0:T(8,128)} %param.8), kind=kLoop, calls=%fused_computation.11 | loop fusion | flops 13762560 | bytes 27525120 | tf_op jit(solution)/shard_map/convert_element_type | solution.py:88
  13.3 5.3 concatenate.3
  18.6 7.6 %all-to-all-start = ((bf16[8,4,2,64,640]{4,3,2,1,0:T(8,128)(2,1)}), bf16[8,4,2,64,640]{4,3,2,1,0:T(8,128)(2,1)}, u32[]{:S(2)}, u32[]{:S(2)}) async-start(bf16[8,4,2,64,640]{4,3,2,1,0:T(8,128)(2,1)} %bitcast.92), calls=%async_computation | async-start | bytes 10485760 | tf_op jit(solution)/shard_map/all_to_all | solution.py:97
  26.2 115.7 %all-to-all-done = bf16[8,4,2,64,640]{4,3,2,1,0:T(8,128)(2,1)} async-done(((bf16[8,4,2,64,640]{4,3,2,1,0:T(8,128)(2,1)}), bf16[8,4,2,64,640]{4,3,2,1,0:T(8,128)(2,1)}, u32[]{:S(2)}, u32[]{:S(2)}) %all-to-all-start) | async-done | bytes 5242912 | tf_op jit(solution)/shard_map/all_to_all | solution.py:97
  141.9 3.1 copy.20
  145.0 0.0 copy-start
  145.0 2.3 copy-done
  147.4 2.0 constant_dynamic-slice_fusion
  149.4 0.0 collective-permute-start
  149.4 1.5 collective-permute-start.1
  150.9 0.3 collective-permute-start.2
  151.3 0.3 squeeze.19
  151.6 1.5 bitcast_dynamic-update-slice_fusion.3
  153.2 0.0 collective-permute-done
  153.2 1.5 bitcast_dynamic-update-slice_fusion.2
  154.7 26.5 %collective-permute-done.1 = bf16[1,1,2,512,640]{4,3,2,1,0:T(8,128)(2,1)S(1)} collective-permute-done((bf16[1,1,2,512,640]{4,3,2,1,0:T(8,128)(2,1)}, bf16[1,1,2,512,640]{4,3,2,1,0:T(8,128)(2,1)S(1)}, u32[]{:S(2)}, u32[]{:S(2)}) %collective-permute-start.1) | collective-permute-done | bytes 1310752 | tf_op jit(solution)/shard_map/ppermute | solution.py:29
  181.2 0.2 bitcast_dynamic-update-slice_fusion.1
  181.4 27.1 %collective-permute-done.2 = bf16[1,1,2,512,640]{4,3,2,1,0:T(8,128)(2,1)S(1)} collective-permute-done((bf16[1,1,2,512,640]{4,3,2,1,0:T(8,128)(2,1)}, bf16[1,1,2,512,640]{4,3,2,1,0:T(8,128)(2,1)S(1)}, u32[]{:S(2)}, u32[]{:S(2)}) %collective-permute-start.2) | collective-permute-done | bytes 1310752 | tf_op jit(solution)/shard_map/ppermute | solution.py:29
  208.5 0.2 bitcast_dynamic-update-slice_fusion
  208.7 1.5 fusion
  210.2 1.2 fusion.1
  211.4 0.0 copy-start.1
  211.4 2.3 copy-done.1
  213.7 2.9 convolution_convert_fusion.4
  216.6 8.4 %add_convert_fusion.4 = bf16[2,512,2560]{2,1,0:T(8,128)(2,1)} fusion(bf16[2,512,2560]{2,1,0:T(8,128)(2,1)} %copy-done.1, bf16[2,512,512]{2,1,0:T(8,128)(2,1)S(1)} %convolution_convert_fusion.4), kind=kOutput, calls=%fused_computation.10 | convolution fusion | flops 3234332672 | bytes 11534336 | tf_op jit(solution)/shard_map/krs,ksc->krc/dot_general | solution.py:54
  225.0 6.9 %convolution_convert_fusion.3 = bf16[2,512,512]{2,1,0:T(8,128)(2,1)S(1)} fusion(bf16[2,512,2560]{2,1,0:T(8,128)(2,1)} %add_convert_fusion.4), kind=kOutput, calls=%fused_computation.22 | convolution fusion | flops 2684878848 | bytes 6291456 | tf_op jit(solution)/shard_map/krc,ksc->krs/dot_general | solution.py:45
  232.0 8.9 %add_convert_fusion.3 = bf16[2,512,2560]{2,1,0:T(8,128)(2,1)} fusion(bf16[2,512,2560]{2,1,0:T(8,128)(2,1)} %add_convert_fusion.4, bf16[2,512,512]{2,1,0:T(8,128)(2,1)S(1)} %convolution_convert_fusion.3), kind=kOutput, calls=%fused_computation.9 | convolution fusion | flops 3234332672 | bytes 11534336 | tf_op jit(solution)/shard_map/krs,ksc->krc/dot_general | solution.py:54
  240.9 7.0 %convolution_convert_fusion.2 = bf16[2,512,512]{2,1,0:T(8,128)(2,1)S(1)} fusion(bf16[2,512,2560]{2,1,0:T(8,128)(2,1)} %add_convert_fusion.3), kind=kOutput, calls=%fused_computation.21 | convolution fusion | flops 2684878848 | bytes 6291456 | tf_op jit(solution)/shard_map/krc,ksc->krs/dot_general | solution.py:45
  247.9 8.4 %add_convert_fusion.2 = bf16[2,512,2560]{2,1,0:T(8,128)(2,1)} fusion(bf16[2,512,2560]{2,1,0:T(8,128)(2,1)} %add_convert_fusion.3, bf16[2,512,512]{2,1,0:T(8,128)(2,1)S(1)} %convolution_convert_fusion.2), kind=kOutput, calls=%fused_computation.8 | convolution fusion | flops 3234332672 | bytes 11534336 | tf_op jit(solution)/shard_map/krs,ksc->krc/dot_general | solution.py:54
  256.3 6.9 %convolution_convert_fusion.1 = bf16[2,512,512]{2,1,0:T(8,128)(2,1)S(1)} fusion(bf16[2,512,2560]{2,1,0:T(8,128)(2,1)} %add_convert_fusion.2), kind=kOutput, calls=%fused_computation.20 | convolution fusion | flops 2684878848 | bytes 6291456 | tf_op jit(solution)/shard_map/krc,ksc->krs/dot_general | solution.py:45
  263.3 8.4 %add_convert_fusion.1 = bf16[2,512,2560]{2,1,0:T(8,128)(2,1)} fusion(bf16[2,512,2560]{2,1,0:T(8,128)(2,1)} %add_convert_fusion.2, bf16[2,512,512]{2,1,0:T(8,128)(2,1)S(1)} %convolution_convert_fusion.1), kind=kOutput, calls=%fused_computation.7 | convolution fusion | flops 3234332672 | bytes 11534336 | tf_op jit(solution)/shard_map/krs,ksc->krc/dot_general | solution.py:54
  271.7 6.9 %convolution_convert_fusion = bf16[2,512,512]{2,1,0:T(8,128)(2,1)S(1)} fusion(bf16[2,512,2560]{2,1,0:T(8,128)(2,1)} %add_convert_fusion.1), kind=kOutput, calls=%fused_computation.19 | convolution fusion | flops 2684878848 | bytes 6291456 | tf_op jit(solution)/shard_map/krc,ksc->krs/dot_general | solution.py:45
  278.7 8.6 %add_convert_fusion = bf16[2,512,2560]{2,1,0:T(8,128)(2,1)} fusion(bf16[2,512,2560]{2,1,0:T(8,128)(2,1)} %add_convert_fusion.1, bf16[2,512,512]{2,1,0:T(8,128)(2,1)S(1)} %convolution_convert_fusion), kind=kOutput, calls=%fused_computation.6 | convolution fusion | flops 3234332672 | bytes 11534336 | tf_op jit(solution)/shard_map/krs,ksc->krc/dot_general | solution.py:54
  287.2 10.2 %copy.21 = bf16[1,1,2,512,2560]{4,2,1,0,3:T(2,128)(2,1)} copy(bf16[1,1,2,512,2560]{4,3,2,1,0:T(8,128)(2,1)} %bitcast.95) | data formatting | bytes 10485760 | tf_op jit(solution)/shard_map/broadcast_in_dim | solution.py:101
  297.5 120.8 %all_to_all.51 = bf16[1,1,2,512,2560]{4,2,1,0,3:T(2,128)(2,1)} all-to-all(bf16[1,1,2,512,2560]{4,2,1,0,3:T(2,128)(2,1)} %copy.21), channel_id=1, replica_groups=mesh['shard'=8,'tensor'=4] {'shard'}, dimensions={3} | all-to-all | bytes 10485760 | tf_op jit(solution)/shard_map/all_to_all | solution.py:101
  418.3 17.4 %copy.22 = bf16[1,1,2,8,64,2560]{4,3,2,5,1,0:T(8,128)(2,1)} copy(bf16[1,1,2,8,64,2560]{5,2,4,3,1,0:T(2,128)(2,1)} %bitcast.93) | data formatting | bytes 10485760 | tf_op jit(solution)/shard_map/all_to_all | solution.py:101
  435.7 10.4 %bitcast_bitcast_fusion = bf16[2560,1,2,8,64]{4,3,2,1,0:T(8,128)(2,1)} fusion(bf16[1,1,2,8,64,2560]{4,3,2,5,1,0:T(8,128)(2,1)} %copy.22), kind=kLoop, calls=%fused_computation.68 | loop fusion | bytes 10485760
  446.1 11.2 %reshape.45 = bf16[4,2,327680]{2,1,0:T(2,128)(2,1)} reshape(bf16[2560,1,2,8,64]{4,3,2,1,0:T(8,128)(2,1)} %bitcast_bitcast_fusion) | data formatting | bytes 10485760
  457.2 0.0 copy-start.3
  457.2 0.0 copy-start.5
  457.2 0.0 copy-start.2
  457.2 0.0 copy-start.4
  457.3 5.5 all-to-all-start.2
  462.8 0.0 copy-done.3
  462.8 0.0 copy-done.5
  462.8 0.2 fusion.19
  463.1 0.9 pad_maximum_fusion.1
  463.9 0.0 copy-done.2
  463.9 0.0 copy-done.4
  463.9 0.5 fusion.10
  464.4 1.1 pad_maximum_fusion
  465.6 56.7 %all-to-all-done.2 = bf16[4,2,327680]{2,1,0:T(2,128)(2,1)} async-done(((bf16[4,2,327680]{2,1,0:T(2,128)(2,1)}), bf16[4,2,327680]{2,1,0:T(2,128)(2,1)}, u32[]{:S(2)}, u32[]{:S(2)}) %all-to-all-start.2) | async-done | bytes 5242912 | tf_op jit(solution)/shard_map/all_to_all | solution.py:100
  522.3 11.0 %reshape.46 = bf16[2560,1,2,8,64]{4,3,2,1,0:T(8,128)(2,1)} reshape(bf16[4,2,327680]{2,1,0:T(2,128)(2,1)} %all-to-all-done.2) | data formatting | bytes 10485760
  533.3 12.7 %copy.24 = bf16[8,1,2,64,4,640]{5,3,2,1,4,0:T(8,128)(2,1)} copy(bf16[8,1,2,64,4,640]{3,0,2,5,4,1:T(8,128)(2,1)} %bitcast.89) | data formatting | bytes 10485760 | tf_op jit(solution)/shard_map/all_to_all | solution.py:100
  546.0 7.1 %convert_multiply_fusion.1 = f32[7,4,1,2,64,640]{5,4,3,2,1,0:T(8,128)} fusion(bf16[8,4,1,2,64,640]{5,4,3,2,1,0:T(8,128)(2,1)} %bitcast.94), kind=kLoop, calls=%fused_computation.13 | loop fusion | flops 4587520 | bytes 13762560 | tf_op jit(solution)/shard_map/mul | solution.py:109
  553.1 12.4 %bitcast_add_fusion = f32[56,64,640]{2,1,0:T(8,128)} fusion(f32[7,4,1,2,64,640]{5,4,3,2,1,0:T(8,128)} %convert_multiply_fusion.1, f32[56,64,640]{2,1,0:T(8,128)} %param.9), kind=kLoop, calls=%fused_computation.12 | loop fusion | flops 4587520 | bytes 27525120 | tf_op jit(solution)/shard_map/add | solution.py:109
  (2 shorter events, 0.0 us)
Async XLA Ops:
  18.6 123.3 %all-to-all-start = ((bf16[8,4,2,64,640]{4,3,2,1,0:T(8,128)(2,1)}), bf16[8,4,2,64,640]{4,3,2,1,0:T(8,128)(2,1)}, u32[]{:S(2)}, u32[]{:S(2)}) async-start(bf16[8,4,2,64,640]{4,3,2,1,0:T(8,128)(2,1)} %bitcast.92), calls=%async_computation | async-start | bytes 10485760 | tf_op jit(solution)/shard_map/all_to_all | solution.py:97
  145.0 2.4 copy-start
  149.4 3.8 collective-permute-start
  149.4 31.8 %collective-permute-start.1 = (bf16[1,1,2,512,640]{4,3,2,1,0:T(8,128)(2,1)}, bf16[1,1,2,512,640]{4,3,2,1,0:T(8,128)(2,1)S(1)}, u32[]{:S(2)}, u32[]{:S(2)}) collective-permute-start(bf16[1,1,2,512,640]{4,3,2,1,0:T(8,128)(2,1)} %get-tuple-element.7), channel_id=1, source_target_pairs={{0,2},{1,3},{2,0},{3,1},{4,6},{5,7},{6,4},{7,5},{8,10},{9,11},{10,... | collective-permute-start | bytes 3932168 | tf_op jit(solution)/shard_map/ppermute | solution.py:29
  150.9 57.6 %collective-permute-start.2 = (bf16[1,1,2,512,640]{4,3,2,1,0:T(8,128)(2,1)}, bf16[1,1,2,512,640]{4,3,2,1,0:T(8,128)(2,1)S(1)}, u32[]{:S(2)}, u32[]{:S(2)}) collective-permute-start(bf16[1,1,2,512,640]{4,3,2,1,0:T(8,128)(2,1)} %get-tuple-element.6), channel_id=1, source_target_pairs={{0,3},{1,2},{2,1},{3,0},{4,7},{5,6},{6,5},{7,4},{8,11},{9,10},{10,... | collective-permute-start | bytes 3932168 | tf_op jit(solution)/shard_map/ppermute | solution.py:29
  211.4 2.4 copy-start.1
  457.2 5.6 copy-start.3
  457.2 5.6 copy-start.5
  457.2 6.7 %copy-start.2 = (f32[3,256,640]{2,1,0:T(8,128)S(1)}, f32[3,256,640]{2,1,0:T(8,128)}, u32[]{:S(2)}) copy-start(f32[3,256,640]{2,1,0:T(8,128)} %param.11) | copy-start | bytes 5898244
  457.2 6.7 %copy-start.4 = (bf16[256,640]{1,0:T(8,128)(2,1)S(1)}, bf16[256,640]{1,0:T(8,128)(2,1)}, u32[]{:S(2)}) copy-start(bf16[256,640]{1,0:T(8,128)(2,1)} %param.10) | copy-start | bytes 983044
  457.3 65.0 %all-to-all-start.2 = ((bf16[4,2,327680]{2,1,0:T(2,128)(2,1)}), bf16[4,2,327680]{2,1,0:T(2,128)(2,1)}, u32[]{:S(2)}, u32[]{:S(2)}) async-start(bf16[4,2,327680]{2,1,0:T(2,128)(2,1)} %reshape.45), calls=%async_computation.2 | async-start | bytes 10485760 | tf_op jit(solution)/shard_map/all_to_all | solution.py:100
